TPU v7x, 32 devices: a whole 2x2x4 slice. The times are simulated.
32 devices in a mesh: slab: 2 (over x), blk: 16 (over z, y, core).
Axes of the slice: x: 2, y: 2, z: 4, core: 2. Of those that a mesh axis runs over, the one named last changes fastest.
Arguments:
- transmit: bfloat16 [2, 1024, 2048], P('slab', 'blk'), may hold values from -0.125 to 0.125
- reflect: bfloat16 [2, 2, 1024, 2048], P('slab', None, 'blk'), may hold values from -0.07910156 to 0.07910156
- source_amp: bfloat16 [512, 2048], P('blk'), may hold values from -6 to 6
- source_cell: int32 [512], P('blk'), may hold values from 0 to 1023
- source_slab: int32 [512], P('blk'), may hold values from 0 to 1
Outputs:
- sweep_out: float32 [2, 512, 2048], P('slab', 'blk')
All inputs are finite; a program needn't handle non-finite values.
Results may differ from a plain program's by a relative error of at most 0.018.
Values may be sent and summed in bfloat16 or wider, within the bound.
A program may use at most 64 MiB of HBM per device.

v0:
```python
import jax
import jax.numpy as jnp
from jax import lax
from jax.sharding import PartitionSpec as P


def shifted(block, axis, distance):
    devices = range(lax.axis_size(axis))
    route = [(i - distance, i) for i in devices if i - distance in devices]
    return lax.ppermute(block, axis, route)


def transposed(matrix):
    half_width = matrix.shape[0]
    return jnp.concatenate([matrix[:, :half_width].T, matrix[:, half_width:].T], 1)


def complex_rows(left_rows, right_matrix):
    inner_width = right_matrix.shape[0]
    outer_width = right_matrix.shape[1] // 2
    row_count = left_rows.shape[0]
    stacked = jnp.concatenate([left_rows[:, :inner_width], left_rows[:, inner_width:]], 0)
    product = jnp.dot(stacked, right_matrix, preferred_element_type=jnp.float32)
    real_out = product[:row_count, :outer_width] - product[row_count:, outer_width:]
    imag_out = product[:row_count, outer_width:] + product[row_count:, :outer_width]
    return jnp.concatenate([real_out, imag_out], 1)


def body(transmit, reflect, source_amp, source_cell, source_slab):
    trans_local = transmit[0]
    refl_local = reflect[0]
    half_width = source_amp.shape[1] // 2
    refl_second = lax.all_gather(refl_local[1], "blk", axis=0, tiled=True)
    coupling = complex_rows(refl_local[0], refl_second).astype(jnp.bfloat16)
    start_rows = trans_local.astype(jnp.float32)
    piece_rows = lax.all_gather(trans_local, "blk", axis=0, tiled=True)
    piece_count = piece_rows.shape[0]
    real_cols = lax.slice_in_dim(coupling, 0, piece_count, axis=1)
    imag_cols = lax.dynamic_slice_in_dim(coupling, half_width, piece_count, 1)
    left_rows = jnp.concatenate([real_cols, imag_cols], 1)
    joined = (start_rows + complex_rows(left_rows, piece_rows)).astype(jnp.bfloat16)
    slab_matrix = lax.all_gather(joined, "blk", axis=0, tiled=True)
    back_matrix = transposed(slab_matrix)
    cell_index = lax.iota(jnp.int32, half_width)
    offset = (cell_index[None, :] - source_cell[:, None]) % half_width
    inside = offset < half_width // 4
    here = source_slab == lax.axis_index("slab")
    keep = inside & here[:, None]
    keep = jnp.concatenate([keep, keep], 1)
    forcing = jnp.where(keep, source_amp, jnp.zeros_like(source_amp))
    chain_length = lax.axis_size("slab")
    carried = forcing
    for sweep_step in range(chain_length - 1):
        arrived = shifted(carried, "slab", 1)
        carried = (forcing.astype(jnp.float32) + complex_rows(arrived, slab_matrix)).astype(
            jnp.bfloat16
        )
    current = carried.astype(jnp.float32)
    for sweep_step in range(chain_length - 1):
        message = complex_rows(current.astype(jnp.bfloat16), back_matrix).astype(jnp.bfloat16)
        arrived = shifted(message, "slab", -1)
        current = carried.astype(jnp.float32) + arrived.astype(jnp.float32)
    return current[None]


def solution(mesh):
    return jax.shard_map(
        body,
        mesh=mesh,
        in_specs=(
            P("slab", "blk", None),
            P("slab", None, "blk", None),
            P("blk", None),
            P("blk"),
            P("blk"),
        ),
        out_specs=P("slab", "blk", None),
        check_vma=False,
    )
```

profile of v0, /device:TPU:0, one launch (start us, length us, event | category | flops | bytes accessed | tf_op | source)
XLA Modules:
  0.0 186.9 jit_solution(4141823036874665269)
XLA Ops:
  6.5 0.0 all-gather.8.cloned.1.call-start
  6.5 1.8 slice_bitcast_fusion.2
  8.3 0.0 all-gather.8.cloned.1.call-update
  8.3 0.0 all-gather.10.cloned.1.call-start
  8.4 0.7 all-gather.10.cloned.1.call-update
  9.1 0.0 all-gather.6.cloned.1.call-start
  9.2 53.5 %all-gather.8.cloned.1.call-done = bf16[1,1,1024,2048]{3,2,1,0:T(8,128)(2,1)} async-done(((bf16[1,1,64,2048]{3,2,1,0:T(8,128)(2,1)}), bf16[1,1,1024,2048]{3,2,1,0:T(8,128)(2,1)}) %all-gather.8.cloned.1.call-update) | async-done | bytes 4194320 | tf_op jit(solution)/shard_map/all_gather | solution.py:33
  62.6 2.9 %fusion.6 = f32[128,2048]{1,0:T(8,128)S(1)} fusion(bf16[1,1,1024,2048]{3,2,1,0:T(8,128)(2,1)} %all-gather.8.cloned.1.call-done, bf16[64,1024]{1,0:T(8,128)(2,1)S(1)} %get-tuple-element.18, bf16[64,1024]{1,0:T(8,128)(2,1)S(1)} %get-tuple-element.17), kind=kOutput, calls=%fused_computation.6 | convolution fusion | flops 537395200 | bytes 5505024 | tf_op jit(solution)/shard_map/dot_general | solution.py:23
  65.5 0.0 copy-start.1
  65.5 0.1 fusion.10
  65.6 48.1 %all-gather.10.cloned.1.call-done = bf16[1,1024,2048]{2,1,0:T(8,128)(2,1)} async-done(((bf16[1,64,2048]{2,1,0:T(8,128)(2,1)}), bf16[1,1024,2048]{2,1,0:T(8,128)(2,1)}) %all-gather.10.cloned.1.call-update) | async-done | bytes 4194320 | tf_op jit(solution)/shard_map/all_gather | solution.py:36
  113.7 0.0 copy-start.4
  113.7 0.0 copy-start.2
  113.7 2.9 %fusion.4 = f32[128,2048]{1,0:T(8,128)S(1)} fusion(bf16[1,1024,2048]{2,1,0:T(8,128)(2,1)} %all-gather.10.cloned.1.call-done, bf16[64,1024]{1,0:T(8,128)(2,1)S(1)} %get-tuple-element.10, bf16[64,1024]{1,0:T(8,128)(2,1)S(1)} %get-tuple-element.9), kind=kOutput, calls=%fused_computation.4 | convolution fusion | flops 537395200 | bytes 5505024 | tf_op jit(solution)/shard_map/dot_general | solution.py:23
  116.7 0.1 slice_subtract_fusion
  116.7 0.0 copy-done.1
  116.8 0.8 fusion.8
  117.5 0.0 all-gather.6.cloned.1.call-update
  117.6 0.0 copy-done.4
  117.6 0.0 copy-done.3
  117.6 0.1 fusion.32
  117.7 0.0 copy-done.2
  117.8 3.4 %collective-permute-start = (bf16[32,2048]{1,0:T(8,128)(2,1)S(1)}, bf16[32,2048]{1,0:T(8,128)(2,1)S(1)}, u32[]{:S(2)}, u32[]{:S(2)}) collective-permute-start(bf16[32,2048]{1,0:T(8,128)(2,1)S(1)} %add_select_fusion), channel_id=1, source_target_pairs={{0,16},{1,17},{2,18},{3,19},{4,20},{5,21},{6,22},{7,23},{8,24},{9,... | collective-permute-start | bytes 393224 | tf_op jit(solution)/shard_map/ppermute | solution.py:10
  121.2 3.1 %collective-permute-done = bf16[32,2048]{1,0:T(8,128)(2,1)S(1)} collective-permute-done((bf16[32,2048]{1,0:T(8,128)(2,1)S(1)}, bf16[32,2048]{1,0:T(8,128)(2,1)S(1)}, u32[]{:S(2)}, u32[]{:S(2)}) %collective-permute-start) | collective-permute-done | bytes 131104 | tf_op jit(solution)/shard_map/ppermute | solution.py:10
  124.3 42.3 %all-gather.6.cloned.1.call-done = bf16[1024,2048]{1,0:T(8,128)(2,1)} async-done(((bf16[64,2048]{1,0:T(8,128)(2,1)}), bf16[1024,2048]{1,0:T(8,128)(2,1)}) %all-gather.6.cloned.1.call-update) | async-done | bytes 4194320 | tf_op jit(solution)/shard_map/all_gather | solution.py:42
  166.6 3.2 %fusion.22 = f32[64,2048]{1,0:T(8,128)S(1)} fusion(bf16[1024,2048]{1,0:T(8,128)(2,1)} %all-gather.6.cloned.1.call-done, bf16[32,1024]{1,0:T(8,128)(2,1)S(1)} %get-tuple-element.22, bf16[32,1024]{1,0:T(8,128)(2,1)S(1)} %get-tuple-element.21), kind=kOutput, calls=%fused_computation.40 | convolution fusion | flops 268697600 | bytes 4849664 | tf_op jit(solution)/shard_map/dot_general | solution.py:23
  169.9 0.2 copy-done
  170.1 0.5 slice_bitcast_fusion.1
  170.6 1.4 fusion
  172.1 1.3 collective-permute-start.1
  173.4 6.2 %collective-permute-done.1 = bf16[32,2048]{1,0:T(8,128)(2,1)S(1)} collective-permute-done((bf16[32,2048]{1,0:T(8,128)(2,1)S(1)}, bf16[32,2048]{1,0:T(8,128)(2,1)S(1)}, u32[]{:S(2)}, u32[]{:S(2)}) %collective-permute-start.1) | collective-permute-done | bytes 131104 | tf_op jit(solution)/shard_map/ppermute | solution.py:10
  179.6 0.7 add_bitcast_fusion
  (11 shorter events, 0.2 us)
Async XLA Ops:
  6.5 56.1 %all-gather.8.cloned.1.call-start = ((), (), s32[]{:S(2)}) async-start(), calls=%async_computation.1 | async-start | bytes 4456448 | tf_op jit(solution)/shard_map/all_gather | solution.py:33
  8.3 105.4 %all-gather.10.cloned.1.call-start = ((), (), s32[]{:S(2)}) async-start(), calls=%async_computation.2 | async-start | bytes 4456448 | tf_op jit(solution)/shard_map/all_gather | solution.py:36
  9.1 157.5 %all-gather.6.cloned.1.call-start = ((), (), s32[]{:S(2)}) async-start(), calls=%async_computation | async-start | bytes 4456448 | tf_op jit(solution)/shard_map/all_gather | solution.py:42
  65.5 51.2 %copy-start.1 = (bf16[1,64,2048]{2,1,0:T(8,128)(2,1)S(1)}, bf16[1,64,2048]{2,1,0:T(8,128)(2,1)}, u32[]{:S(2)}) copy-start(bf16[1,64,2048]{2,1,0:T(8,128)(2,1)} %param.5) | copy-start | bytes 786436
  113.7 3.8 %copy-start.4 = (s32[32]{0:T(128)S(1)}, s32[32]{0:T(128)}, u32[]{:S(2)}) copy-start(s32[32]{0:T(128)} %param.9) | copy-start | bytes 388
  113.7 3.9 %copy-start.3 = (s32[32]{0:T(128)S(1)}, s32[32]{0:T(128)}, u32[]{:S(2)}) copy-start(s32[32]{0:T(128)} %param.8) | copy-start | bytes 388
  113.7 4.0 %copy-start.2 = (bf16[32,2048]{1,0:T(8,128)(2,1)S(1)}, bf16[32,2048]{1,0:T(8,128)(2,1)}, u32[]{:S(2)}) copy-start(bf16[32,2048]{1,0:T(8,128)(2,1)} %param.7) | copy-start | bytes 393220
  117.8 6.5 %collective-permute-start = (bf16[32,2048]{1,0:T(8,128)(2,1)S(1)}, bf16[32,2048]{1,0:T(8,128)(2,1)S(1)}, u32[]{:S(2)}, u32[]{:S(2)}) collective-permute-start(bf16[32,2048]{1,0:T(8,128)(2,1)S(1)} %add_select_fusion), channel_id=1, source_target_pairs={{0,16},{1,17},{2,18},{3,19},{4,20},{5,21},{6,22},{7,23},{8,24},{9,... | collective-permute-start | bytes 393224 | tf_op jit(solution)/shard_map/ppermute | solution.py:10
  166.6 3.4 %copy-start = (bf16[1024,2048]{1,0:T(8,128)(2,1)S(1)}, bf16[1024,2048]{1,0:T(8,128)(2,1)}, u32[]{:S(2)}) copy-start(bf16[1024,2048]{1,0:T(8,128)(2,1)} %all-gather.6.cloned.1.call-done) | copy-start | bytes 12582916
  172.1 7.5 %collective-permute-start.1 = (bf16[32,2048]{1,0:T(8,128)(2,1)S(1)}, bf16[32,2048]{1,0:T(8,128)(2,1)S(1)}, u32[]{:S(2)}, u32[]{:S(2)}) collective-permute-start(bf16[32,2048]{1,0:T(8,128)(2,1)S(1)} %pad_maximum_fusion), channel_id=1, source_target_pairs={{16,0},{17,1},{18,2},{19,3},{20,4},{21,5},{22,6},{23,7},{24,8},{25... | collective-permute-start | bytes 393224 | tf_op jit(solution)/shard_map/ppermute | solution.py:10
Sparse Core Ops, SparseCore 0:
  9.5 53.0 all-gather.7
  64.8 48.8 all-gather.9
  117.7 48.8 all-gather.5
where the time goes:
time: 187 us
  waiting for transfers between devices  154 us (82%)
  between operations  13.3 us (7%)
  matrix products  10.4 us (6%)
  starting transfers between devices  4.75 us (3%)
  local copies, waits for them, and re-layouts  2.53 us (1%)
  other arithmetic  1.89 us (1%)
    all_gather x1, waiting for transfers between devices, body(): refl_second = lax.all_gather(refl_local[1], 'blk', axis=0, tiled=True)  53.5 us
    all_gather x1, waiting for transfers between devices, body(): piece_rows = lax.all_gather(trans_local, 'blk', axis=0, tiled=True)  48.1 us
    all_gather x1, waiting for transfers between devices, body(): slab_matrix = lax.all_gather(joined, 'blk', axis=0, tiled=True)  42.3 us
    dot_general x4, matrix products, complex_rows(): product = jnp.dot(stacked, right_matrix, preferred_element_type=jnp.float32)  10.4 us
    ppermute x2, waiting for transfers between devices, shifted(): return lax.ppermute(block, axis, route)  9.38 us
    ppermute x2, starting transfers between devices, shifted(): return lax.ppermute(block, axis, route)  4.67 us
  transfers between devices with their start and end apart: 5, of which 5 were waited for; matrix products, arithmetic and copies ran while one was open for 2% of the time, Pallas kernels for 0%

commit v1 on v0

--- a/solution.py
+++ b/solution.py
@@ -33,7 +33,21 @@
     refl_second = lax.all_gather(refl_local[1], "blk", axis=0, tiled=True)
     coupling = complex_rows(refl_local[0], refl_second).astype(jnp.bfloat16)
     start_rows = trans_local.astype(jnp.float32)
-    piece_rows = lax.all_gather(trans_local, "blk", axis=0, tiled=True)
+    ways, here_2, hop = (lax.axis_size("blk"), lax.axis_index("blk"), trans_local.shape[0])
+    shape = [n * ways if d == 0 else n for d, n in enumerate(trans_local.shape)]
+    full = lax.dynamic_update_slice_in_dim(
+        jnp.zeros(shape, trans_local.dtype), trans_local, here_2 * hop, axis=0
+    )
+    going_up = going_down = trans_local
+    for far in range(1, ways // 2 + 1):
+        going_up = lax.ppermute(going_up, "blk", [(d, (d + 1) % ways) for d in range(ways)])
+        full = lax.dynamic_update_slice_in_dim(full, going_up, (here_2 - far) % ways * hop, axis=0)
+        if 2 * far < ways:
+            going_down = lax.ppermute(going_down, "blk", [(d, (d - 1) % ways) for d in range(ways)])
+            full = lax.dynamic_update_slice_in_dim(
+                full, going_down, (here_2 + far) % ways * hop, axis=0
+            )
+    piece_rows = full
     piece_count = piece_rows.shape[0]
     real_cols = lax.slice_in_dim(coupling, 0, piece_count, axis=1)
     imag_cols = lax.dynamic_slice_in_dim(coupling, half_width, piece_count, 1)

time: 187 us -> 164 us (0.88)
  waiting for transfers between devices: 154 us -> 83 us
  starting transfers between devices: 4.75 us -> 38 us
  local copies, waits for them, and re-layouts: 2.53 us -> 16.8 us
    all_gather x1, waiting for transfers between devices: 53.5 us -> 0.01 us  [body(): refl_second = lax.all_gather(refl_local[1], 'blk', axis=0, tiled=True)]
    all_gather x1 -> x0, waiting for transfers between devices: 48.1 us -> none  [body(): piece_rows = lax.all_gather(trans_local, 'blk', axis=0, tiled=True)]
    ppermute x0 -> x15, starting transfers between devices: none -> 34.5 us  [the longest x7 32.4 us: body(): lax.ppermute(going_down, 'blk', [(d, (d - 1) % ways) for d in range(ways)])]
    ppermute x0 -> x15, waiting for transfers between devices: none -> 32.6 us  [the longest x8 19.5 us: body(): lax.ppermute(going_up, 'blk', [(d, (d + 1) % ways) for d in range(ways)])]
    dynamic_update_slice x0 -> x16, local copies, waits for them, and re-layouts: none -> 11.7 us  [the longest x8 5.84 us: body(): lax.dynamic_update_slice_in_dim(full, going_up, (here_2 - far) % ways * h...]
    broadcast_in_dim x0 -> x1, local copies, waits for them, and re-layouts: none -> 2.55 us  [body(): jnp.zeros(shape, trans_local.dtype)]
  transfers between devices with their start and end apart: 5 -> 19, of which waited for: 5 -> 14; matrix products, arithmetic and copies ran while one was open for 2% -> 9% of each run, Pallas kernels for 0% -> 0%
where the time goes in v1:
time: 164 us
  waiting for transfers between devices  83 us (51%)
  starting transfers between devices  38 us (23%)
  local copies, waits for them, and re-layouts  16.8 us (10%)
  between operations  13.6 us (8%)
  matrix products  10.4 us (6%)
  other arithmetic  1.89 us (1%)
    all_gather x1, waiting for transfers between devices, body(): slab_matrix = lax.all_gather(joined, 'blk', axis=0, tiled=True)  41.6 us
    ppermute x7, starting transfers between devices, body(): lax.ppermute(going_down, 'blk', [(d, (d - 1) % ways) for d in range(ways)])  32.4 us
    ppermute x8, waiting for transfers between devices, body(): lax.ppermute(going_up, 'blk', [(d, (d + 1) % ways) for d in range(ways)])  19.5 us
    ppermute x7, waiting for transfers between devices, body(): lax.ppermute(going_down, 'blk', [(d, (d - 1) % ways) for d in range(ways)])  13.1 us
    dot_general x4, matrix products, complex_rows(): product = jnp.dot(stacked, right_matrix, preferred_element_type=jnp.float32)  10.4 us
    ppermute x2, waiting for transfers between devices, shifted(): return lax.ppermute(block, axis, route)  8.74 us
    dynamic_update_slice x8, local copies, waits for them, and re-layouts, body(): lax.dynamic_update_slice_in_dim(full, going_up, (here_2 - far) % ways * h...  5.84 us
    dynamic_update_slice x7, local copies, waits for them, and re-layouts, body(): lax.dynamic_update_slice_in_dim(full, going_down, (here_2 + far) % ways *...  5.07 us
  transfers between devices with their start and end apart: 19, of which 14 were waited for; matrix products, arithmetic and copies ran while one was open for 9% of the time, Pallas kernels for 0%

profile of v1, /device:TPU:0, one launch (start us, length us, event | category | flops | bytes accessed | tf_op | source)
XLA Modules:
  0.0 163.7 jit_solution(5955358650885091420)
XLA Ops:
  6.5 1.8 %slice_bitcast_fusion.2 = (bf16[64,2048]{1,0:T(8,128)(2,1)S(1)}, bf16[1,1,64,2048]{3,2,1,0:T(8,128)(2,1)}) fusion(bf16[1,2,64,2048]{3,2,1,0:T(8,128)(2,1)} %param.6), kind=kLoop, calls=%fused_computation.26 | loop fusion | bytes 1048576 | tf_op jit(solution)/shard_map/squeeze | solution.py:34
  9.0 5.0 %collective-permute-start.2 = (bf16[64,2048]{1,0:T(8,128)(2,1)}, bf16[64,2048]{1,0:T(8,128)(2,1)S(1)}, u32[]{:S(2)}, u32[]{:S(2)}) collective-permute-start(bf16[64,2048]{1,0:T(8,128)(2,1)} %bitcast.17), channel_id=1, source_target_pairs={{0,15},{1,0},{2,1},{3,2},{4,3},{5,4},{6,5},{7,6},{8,7},{9,8},{10,9... | collective-permute-start | bytes 786440 | tf_op jit(solution)/shard_map/ppermute | solution.py:46
  14.0 2.6 %broadcast_in_dim.13 = bf16[1024,2048]{1,0:T(8,128)(2,1)} broadcast(bf16[]{:T(256)} %constant.111.clone.1), dimensions={} | broadcast | bytes 4194306 | tf_op jit(solution)/shard_map/broadcast_in_dim | solution.py:39
  17.3 1.0 collective-permute-done.1
  18.3 4.4 %collective-permute-start.4 = (bf16[64,2048]{1,0:T(8,128)(2,1)S(1)}, bf16[64,2048]{1,0:T(8,128)(2,1)S(1)}, u32[]{:S(2)}, u32[]{:S(2)}) collective-permute-start(bf16[64,2048]{1,0:T(8,128)(2,1)S(1)} %collective-permute-done.2), channel_id=1, source_target_pairs={{0,15},{1,0},{2,1},{3,2},{4,3},{5,4},{6,5},{7,6},{8,7},{9,8},{10,9... | collective-permute-start | bytes 786440 | tf_op jit(solution)/shard_map/ppermute | solution.py:46
  24.2 4.5 %collective-permute-done.3 = bf16[64,2048]{1,0:T(8,128)(2,1)S(1)} collective-permute-done((bf16[64,2048]{1,0:T(8,128)(2,1)S(1)}, bf16[64,2048]{1,0:T(8,128)(2,1)S(1)}, u32[]{:S(2)}, u32[]{:S(2)}) %collective-permute-start.3) | collective-permute-done | bytes 262176 | tf_op jit(solution)/shard_map/ppermute | solution.py:43
  28.8 4.4 %collective-permute-start.6 = (bf16[64,2048]{1,0:T(8,128)(2,1)S(1)}, bf16[64,2048]{1,0:T(8,128)(2,1)S(1)}, u32[]{:S(2)}, u32[]{:S(2)}) collective-permute-start(bf16[64,2048]{1,0:T(8,128)(2,1)S(1)} %collective-permute-done.4), channel_id=1, source_target_pairs={{0,15},{1,0},{2,1},{3,2},{4,3},{5,4},{6,5},{7,6},{8,7},{9,8},{10,9... | collective-permute-start | bytes 786440 | tf_op jit(solution)/shard_map/ppermute | solution.py:46
  34.6 3.7 %collective-permute-done.5 = bf16[64,2048]{1,0:T(8,128)(2,1)S(1)} collective-permute-done((bf16[64,2048]{1,0:T(8,128)(2,1)S(1)}, bf16[64,2048]{1,0:T(8,128)(2,1)S(1)}, u32[]{:S(2)}, u32[]{:S(2)}) %collective-permute-start.5) | collective-permute-done | bytes 262176 | tf_op jit(solution)/shard_map/ppermute | solution.py:43
  38.4 4.4 %collective-permute-start.8 = (bf16[64,2048]{1,0:T(8,128)(2,1)S(1)}, bf16[64,2048]{1,0:T(8,128)(2,1)S(1)}, u32[]{:S(2)}, u32[]{:S(2)}) collective-permute-start(bf16[64,2048]{1,0:T(8,128)(2,1)S(1)} %collective-permute-done.6), channel_id=1, source_target_pairs={{0,15},{1,0},{2,1},{3,2},{4,3},{5,4},{6,5},{7,6},{8,7},{9,8},{10,9... | collective-permute-start | bytes 786440 | tf_op jit(solution)/shard_map/ppermute | solution.py:46
  42.8 0.8 constant_dynamic-update-slice_fusion.10
  44.3 2.7 %collective-permute-done.7 = bf16[64,2048]{1,0:T(8,128)(2,1)S(1)} collective-permute-done((bf16[64,2048]{1,0:T(8,128)(2,1)S(1)}, bf16[64,2048]{1,0:T(8,128)(2,1)S(1)}, u32[]{:S(2)}, u32[]{:S(2)}) %collective-permute-start.7) | collective-permute-done | bytes 262176 | tf_op jit(solution)/shard_map/ppermute | solution.py:43
  47.0 5.2 %collective-permute-done.8 = bf16[64,2048]{1,0:T(8,128)(2,1)S(1)} collective-permute-done((bf16[64,2048]{1,0:T(8,128)(2,1)S(1)}, bf16[64,2048]{1,0:T(8,128)(2,1)S(1)}, u32[]{:S(2)}, u32[]{:S(2)}) %collective-permute-start.8) | collective-permute-done | bytes 262176 | tf_op jit(solution)/shard_map/ppermute | solution.py:46
  52.2 4.6 %collective-permute-start.10 = (bf16[64,2048]{1,0:T(8,128)(2,1)S(1)}, bf16[64,2048]{1,0:T(8,128)(2,1)S(1)}, u32[]{:S(2)}, u32[]{:S(2)}) collective-permute-start(bf16[64,2048]{1,0:T(8,128)(2,1)S(1)} %collective-permute-done.8), channel_id=1, source_target_pairs={{0,15},{1,0},{2,1},{3,2},{4,3},{5,4},{6,5},{7,6},{8,7},{9,8},{10,9... | collective-permute-start | bytes 786440 | tf_op jit(solution)/shard_map/ppermute | solution.py:46
  58.3 0.9 collective-permute-done.9
  59.2 1.5 collective-permute-done.10
  60.7 4.8 %collective-permute-start.12 = (bf16[64,2048]{1,0:T(8,128)(2,1)S(1)}, bf16[64,2048]{1,0:T(8,128)(2,1)S(1)}, u32[]{:S(2)}, u32[]{:S(2)}) collective-permute-start(bf16[64,2048]{1,0:T(8,128)(2,1)S(1)} %collective-permute-done.10), channel_id=1, source_target_pairs={{0,15},{1,0},{2,1},{3,2},{4,3},{5,4},{6,5},{7,6},{8,7},{9,8},{10,9... | collective-permute-start | bytes 786440 | tf_op jit(solution)/shard_map/ppermute | solution.py:46
  67.0 1.3 collective-permute-done.11
  68.3 1.6 collective-permute-start.13
  69.9 4.7 %collective-permute-done.12 = bf16[64,2048]{1,0:T(8,128)(2,1)S(1)} collective-permute-done((bf16[64,2048]{1,0:T(8,128)(2,1)S(1)}, bf16[64,2048]{1,0:T(8,128)(2,1)S(1)}, u32[]{:S(2)}, u32[]{:S(2)}) %collective-permute-start.12) | collective-permute-done | bytes 262176 | tf_op jit(solution)/shard_map/ppermute | solution.py:46
  74.5 4.6 %collective-permute-start.14 = (bf16[64,2048]{1,0:T(8,128)(2,1)S(1)}, bf16[64,2048]{1,0:T(8,128)(2,1)S(1)}, u32[]{:S(2)}, u32[]{:S(2)}) collective-permute-start(bf16[64,2048]{1,0:T(8,128)(2,1)S(1)} %collective-permute-done.12), channel_id=1, source_target_pairs={{0,15},{1,0},{2,1},{3,2},{4,3},{5,4},{6,5},{7,6},{8,7},{9,8},{10,9... | collective-permute-start | bytes 786440 | tf_op jit(solution)/shard_map/ppermute | solution.py:46
  81.3 1.7 %collective-permute-done.14 = bf16[64,2048]{1,0:T(8,128)(2,1)S(1)} collective-permute-done((bf16[64,2048]{1,0:T(8,128)(2,1)S(1)}, bf16[64,2048]{1,0:T(8,128)(2,1)S(1)}, u32[]{:S(2)}, u32[]{:S(2)}) %collective-permute-start.14) | collective-permute-done | bytes 262176 | tf_op jit(solution)/shard_map/ppermute | solution.py:46
  83.7 5.3 %collective-permute-done.15 = bf16[64,2048]{1,0:T(8,128)(2,1)S(1)} collective-permute-done((bf16[64,2048]{1,0:T(8,128)(2,1)S(1)}, bf16[64,2048]{1,0:T(8,128)(2,1)S(1)}, u32[]{:S(2)}, u32[]{:S(2)}) %collective-permute-start.15) | collective-permute-done | bytes 262176 | tf_op jit(solution)/shard_map/ppermute | solution.py:43
  89.8 2.9 %fusion.4 = f32[128,2048]{1,0:T(8,128)S(1)} fusion(bf16[1,1,1024,2048]{3,2,1,0:T(8,128)(2,1)} %all-gather.6.cloned.1.call-done, bf16[64,1024]{1,0:T(8,128)(2,1)S(1)} %get-tuple-element.18, bf16[64,1024]{1,0:T(8,128)(2,1)S(1)} %get-tuple-element.17), kind=kOutput, calls=%fused_computation.4 | convolution fusion | flops 537395200 | bytes 5505024 | tf_op jit(solution)/shard_map/dot_general | solution.py:23
  92.8 3.0 %fusion.12 = f32[128,2048]{1,0:T(8,128)S(1)} fusion(bf16[1024,2048]{1,0:T(8,128)(2,1)} %constant_dynamic-update-slice_fusion, bf16[64,1024]{1,0:T(8,128)(2,1)S(1)} %get-tuple-element.10, bf16[64,1024]{1,0:T(8,128)(2,1)S(1)} %get-tuple-element.9), kind=kOutput, calls=%fused_computation.19 | convolution fusion | flops 537395200 | bytes 5505024 | tf_op jit(solution)/shard_map/dot_general | solution.py:23
  95.8 0.8 fusion.6
  96.8 2.1 %collective-permute-start = (bf16[32,2048]{1,0:T(8,128)(2,1)S(1)}, bf16[32,2048]{1,0:T(8,128)(2,1)S(1)}, u32[]{:S(2)}, u32[]{:S(2)}) collective-permute-start(bf16[32,2048]{1,0:T(8,128)(2,1)S(1)} %add_select_fusion), channel_id=1, source_target_pairs={{0,16},{1,17},{2,18},{3,19},{4,20},{5,21},{6,22},{7,23},{8,24},{9,... | collective-permute-start | bytes 393224 | tf_op jit(solution)/shard_map/ppermute | solution.py:10
  99.0 2.5 %collective-permute-done = bf16[32,2048]{1,0:T(8,128)(2,1)S(1)} collective-permute-done((bf16[32,2048]{1,0:T(8,128)(2,1)S(1)}, bf16[32,2048]{1,0:T(8,128)(2,1)S(1)}, u32[]{:S(2)}, u32[]{:S(2)}) %collective-permute-start) | collective-permute-done | bytes 131104 | tf_op jit(solution)/shard_map/ppermute | solution.py:10
  101.5 41.6 %all-gather.4.cloned.1.call-done = bf16[1024,2048]{1,0:T(8,128)(2,1)} async-done(((bf16[64,2048]{1,0:T(8,128)(2,1)}), bf16[1024,2048]{1,0:T(8,128)(2,1)}) %all-gather.4.cloned.1.call-update) | async-done | bytes 4194320 | tf_op jit(solution)/shard_map/all_gather | solution.py:56
  143.1 3.2 %fusion.21 = f32[64,2048]{1,0:T(8,128)S(1)} fusion(bf16[1024,2048]{1,0:T(8,128)(2,1)} %all-gather.4.cloned.1.call-done, bf16[32,1024]{1,0:T(8,128)(2,1)S(1)} %get-tuple-element.22, bf16[32,1024]{1,0:T(8,128)(2,1)S(1)} %get-tuple-element.21), kind=kOutput, calls=%fused_computation.39 | convolution fusion | flops 268697600 | bytes 4849664 | tf_op jit(solution)/shard_map/dot_general | solution.py:23
  147.1 1.4 fusion
  148.6 1.3 collective-permute-start.16
  149.9 6.2 %collective-permute-done.16 = bf16[32,2048]{1,0:T(8,128)(2,1)S(1)} collective-permute-done((bf16[32,2048]{1,0:T(8,128)(2,1)S(1)}, bf16[32,2048]{1,0:T(8,128)(2,1)S(1)}, u32[]{:S(2)}, u32[]{:S(2)}) %collective-permute-start.16) | collective-permute-done | bytes 131104 | tf_op jit(solution)/shard_map/ppermute | solution.py:10
  (55 shorter events, 13.4 us)
Async XLA Ops:
  6.5 10.0 %copy-start.1 = (bf16[1,64,2048]{2,1,0:T(8,128)(2,1)S(1)}, bf16[1,64,2048]{2,1,0:T(8,128)(2,1)}, u32[]{:S(2)}) copy-start(bf16[1,64,2048]{2,1,0:T(8,128)(2,1)} %param.5) | copy-start | bytes 786436
  6.5 83.2 %all-gather.6.cloned.1.call-start = ((), (), s32[]{:S(2)}) async-start(), calls=%async_computation.1 | async-start | bytes 4456448 | tf_op jit(solution)/shard_map/all_gather | solution.py:33
  8.4 134.8 %all-gather.4.cloned.1.call-start = ((), (), s32[]{:S(2)}) async-start(), calls=%async_computation | async-start | bytes 4456448 | tf_op jit(solution)/shard_map/all_gather | solution.py:56
  8.4 9.9 %collective-permute-start.1 = (bf16[64,2048]{1,0:T(8,128)(2,1)}, bf16[64,2048]{1,0:T(8,128)(2,1)S(1)}, u32[]{:S(2)}, u32[]{:S(2)}) collective-permute-start(bf16[64,2048]{1,0:T(8,128)(2,1)} %bitcast.16), channel_id=1, source_target_pairs={{0,1},{1,2},{2,3},{3,4},{4,5},{5,6},{6,7},{7,8},{8,9},{9,10},{10,1... | collective-permute-start | bytes 786440 | tf_op jit(solution)/shard_map/ppermute | solution.py:43
  9.0 9.4 %collective-permute-start.2 = (bf16[64,2048]{1,0:T(8,128)(2,1)}, bf16[64,2048]{1,0:T(8,128)(2,1)S(1)}, u32[]{:S(2)}, u32[]{:S(2)}) collective-permute-start(bf16[64,2048]{1,0:T(8,128)(2,1)} %bitcast.17), channel_id=1, source_target_pairs={{0,15},{1,0},{2,1},{3,2},{4,3},{5,4},{6,5},{7,6},{8,7},{9,8},{10,9... | collective-permute-start | bytes 786440 | tf_op jit(solution)/shard_map/ppermute | solution.py:46
  18.3 10.4 %collective-permute-start.3 = (bf16[64,2048]{1,0:T(8,128)(2,1)S(1)}, bf16[64,2048]{1,0:T(8,128)(2,1)S(1)}, u32[]{:S(2)}, u32[]{:S(2)}) collective-permute-start(bf16[64,2048]{1,0:T(8,128)(2,1)S(1)} %collective-permute-done.1), channel_id=1, source_target_pairs={{0,1},{1,2},{2,3},{3,4},{4,5},{5,6},{6,7},{7,8},{8,9},{9,10},{10,1... | collective-permute-start | bytes 786440 | tf_op jit(solution)/shard_map/ppermute | solution.py:43
  18.3 10.4 %collective-permute-start.4 = (bf16[64,2048]{1,0:T(8,128)(2,1)S(1)}, bf16[64,2048]{1,0:T(8,128)(2,1)S(1)}, u32[]{:S(2)}, u32[]{:S(2)}) collective-permute-start(bf16[64,2048]{1,0:T(8,128)(2,1)S(1)} %collective-permute-done.2), channel_id=1, source_target_pairs={{0,15},{1,0},{2,1},{3,2},{4,3},{5,4},{6,5},{7,6},{8,7},{9,8},{10,9... | collective-permute-start | bytes 786440 | tf_op jit(solution)/shard_map/ppermute | solution.py:46
  28.8 9.6 %collective-permute-start.5 = (bf16[64,2048]{1,0:T(8,128)(2,1)S(1)}, bf16[64,2048]{1,0:T(8,128)(2,1)S(1)}, u32[]{:S(2)}, u32[]{:S(2)}) collective-permute-start(bf16[64,2048]{1,0:T(8,128)(2,1)S(1)} %collective-permute-done.3), channel_id=1, source_target_pairs={{0,1},{1,2},{2,3},{3,4},{4,5},{5,6},{6,7},{7,8},{8,9},{9,10},{10,1... | collective-permute-start | bytes 786440 | tf_op jit(solution)/shard_map/ppermute | solution.py:43
  28.8 9.6 %collective-permute-start.6 = (bf16[64,2048]{1,0:T(8,128)(2,1)S(1)}, bf16[64,2048]{1,0:T(8,128)(2,1)S(1)}, u32[]{:S(2)}, u32[]{:S(2)}) collective-permute-start(bf16[64,2048]{1,0:T(8,128)(2,1)S(1)} %collective-permute-done.4), channel_id=1, source_target_pairs={{0,15},{1,0},{2,1},{3,2},{4,3},{5,4},{6,5},{7,6},{8,7},{9,8},{10,9... | collective-permute-start | bytes 786440 | tf_op jit(solution)/shard_map/ppermute | solution.py:46
  38.4 8.6 %collective-permute-start.7 = (bf16[64,2048]{1,0:T(8,128)(2,1)S(1)}, bf16[64,2048]{1,0:T(8,128)(2,1)S(1)}, u32[]{:S(2)}, u32[]{:S(2)}) collective-permute-start(bf16[64,2048]{1,0:T(8,128)(2,1)S(1)} %collective-permute-done.5), channel_id=1, source_target_pairs={{0,1},{1,2},{2,3},{3,4},{4,5},{5,6},{6,7},{7,8},{8,9},{9,10},{10,1... | collective-permute-start | bytes 786440 | tf_op jit(solution)/shard_map/ppermute | solution.py:43
  38.4 13.8 %collective-permute-start.8 = (bf16[64,2048]{1,0:T(8,128)(2,1)S(1)}, bf16[64,2048]{1,0:T(8,128)(2,1)S(1)}, u32[]{:S(2)}, u32[]{:S(2)}) collective-permute-start(bf16[64,2048]{1,0:T(8,128)(2,1)S(1)} %collective-permute-done.6), channel_id=1, source_target_pairs={{0,15},{1,0},{2,1},{3,2},{4,3},{5,4},{6,5},{7,6},{8,7},{9,8},{10,9... | collective-permute-start | bytes 786440 | tf_op jit(solution)/shard_map/ppermute | solution.py:46
  47.0 12.2 %collective-permute-start.9 = (bf16[64,2048]{1,0:T(8,128)(2,1)S(1)}, bf16[64,2048]{1,0:T(8,128)(2,1)S(1)}, u32[]{:S(2)}, u32[]{:S(2)}) collective-permute-start(bf16[64,2048]{1,0:T(8,128)(2,1)S(1)} %collective-permute-done.7), channel_id=1, source_target_pairs={{0,1},{1,2},{2,3},{3,4},{4,5},{5,6},{6,7},{7,8},{8,9},{9,10},{10,1... | collective-permute-start | bytes 786440 | tf_op jit(solution)/shard_map/ppermute | solution.py:43
  52.2 8.5 %collective-permute-start.10 = (bf16[64,2048]{1,0:T(8,128)(2,1)S(1)}, bf16[64,2048]{1,0:T(8,128)(2,1)S(1)}, u32[]{:S(2)}, u32[]{:S(2)}) collective-permute-start(bf16[64,2048]{1,0:T(8,128)(2,1)S(1)} %collective-permute-done.8), channel_id=1, source_target_pairs={{0,15},{1,0},{2,1},{3,2},{4,3},{5,4},{6,5},{7,6},{8,7},{9,8},{10,9... | collective-permute-start | bytes 786440 | tf_op jit(solution)/shard_map/ppermute | solution.py:46
  59.2 9.1 %collective-permute-start.11 = (bf16[64,2048]{1,0:T(8,128)(2,1)S(1)}, bf16[64,2048]{1,0:T(8,128)(2,1)S(1)}, u32[]{:S(2)}, u32[]{:S(2)}) collective-permute-start(bf16[64,2048]{1,0:T(8,128)(2,1)S(1)} %collective-permute-done.9), channel_id=1, source_target_pairs={{0,1},{1,2},{2,3},{3,4},{4,5},{5,6},{6,7},{7,8},{8,9},{9,10},{10,1... | collective-permute-start | bytes 786440 | tf_op jit(solution)/shard_map/ppermute | solution.py:43
  60.7 13.8 %collective-permute-start.12 = (bf16[64,2048]{1,0:T(8,128)(2,1)S(1)}, bf16[64,2048]{1,0:T(8,128)(2,1)S(1)}, u32[]{:S(2)}, u32[]{:S(2)}) collective-permute-start(bf16[64,2048]{1,0:T(8,128)(2,1)S(1)} %collective-permute-done.10), channel_id=1, source_target_pairs={{0,15},{1,0},{2,1},{3,2},{4,3},{5,4},{6,5},{7,6},{8,7},{9,8},{10,9... | collective-permute-start | bytes 786440 | tf_op jit(solution)/shard_map/ppermute | solution.py:46
  68.3 12.3 %collective-permute-start.13 = (bf16[64,2048]{1,0:T(8,128)(2,1)S(1)}, bf16[64,2048]{1,0:T(8,128)(2,1)S(1)}, u32[]{:S(2)}, u32[]{:S(2)}) collective-permute-start(bf16[64,2048]{1,0:T(8,128)(2,1)S(1)} %collective-permute-done.11), channel_id=1, source_target_pairs={{0,1},{1,2},{2,3},{3,4},{4,5},{5,6},{6,7},{7,8},{8,9},{9,10},{10,1... | collective-permute-start | bytes 786440 | tf_op jit(solution)/shard_map/ppermute | solution.py:43
  74.5 8.5 %collective-permute-start.14 = (bf16[64,2048]{1,0:T(8,128)(2,1)S(1)}, bf16[64,2048]{1,0:T(8,128)(2,1)S(1)}, u32[]{:S(2)}, u32[]{:S(2)}) collective-permute-start(bf16[64,2048]{1,0:T(8,128)(2,1)S(1)} %collective-permute-done.12), channel_id=1, source_target_pairs={{0,15},{1,0},{2,1},{3,2},{4,3},{5,4},{6,5},{7,6},{8,7},{9,8},{10,9... | collective-permute-start | bytes 786440 | tf_op jit(solution)/shard_map/ppermute | solution.py:46
  80.6 8.5 %collective-permute-start.15 = (bf16[64,2048]{1,0:T(8,128)(2,1)S(1)}, bf16[64,2048]{1,0:T(8,128)(2,1)S(1)}, u32[]{:S(2)}, u32[]{:S(2)}) collective-permute-start(bf16[64,2048]{1,0:T(8,128)(2,1)S(1)} %collective-permute-done.13), channel_id=1, source_target_pairs={{0,1},{1,2},{2,3},{3,4},{4,5},{5,6},{6,7},{7,8},{8,9},{9,10},{10,1... | collective-permute-start | bytes 786440 | tf_op jit(solution)/shard_map/ppermute | solution.py:43
  92.8 3.9 %copy-start.4 = (s32[32]{0:T(128)S(1)}, s32[32]{0:T(128)}, u32[]{:S(2)}) copy-start(s32[32]{0:T(128)} %param.9) | copy-start | bytes 388
  92.8 3.9 %copy-start.3 = (s32[32]{0:T(128)S(1)}, s32[32]{0:T(128)}, u32[]{:S(2)}) copy-start(s32[32]{0:T(128)} %param.8) | copy-start | bytes 388
  92.8 4.0 %copy-start.2 = (bf16[32,2048]{1,0:T(8,128)(2,1)S(1)}, bf16[32,2048]{1,0:T(8,128)(2,1)}, u32[]{:S(2)}) copy-start(bf16[32,2048]{1,0:T(8,128)(2,1)} %param.7) | copy-start | bytes 393220
  96.8 4.6 %collective-permute-start = (bf16[32,2048]{1,0:T(8,128)(2,1)S(1)}, bf16[32,2048]{1,0:T(8,128)(2,1)S(1)}, u32[]{:S(2)}, u32[]{:S(2)}) collective-permute-start(bf16[32,2048]{1,0:T(8,128)(2,1)S(1)} %add_select_fusion), channel_id=1, source_target_pairs={{0,16},{1,17},{2,18},{3,19},{4,20},{5,21},{6,22},{7,23},{8,24},{9,... | collective-permute-start | bytes 393224 | tf_op jit(solution)/shard_map/ppermute | solution.py:10
  143.1 3.4 %copy-start = (bf16[1024,2048]{1,0:T(8,128)(2,1)S(1)}, bf16[1024,2048]{1,0:T(8,128)(2,1)}, u32[]{:S(2)}) copy-start(bf16[1024,2048]{1,0:T(8,128)(2,1)} %all-gather.4.cloned.1.call-done) | copy-start | bytes 12582916
  148.6 7.5 %collective-permute-start.16 = (bf16[32,2048]{1,0:T(8,128)(2,1)S(1)}, bf16[32,2048]{1,0:T(8,128)(2,1)S(1)}, u32[]{:S(2)}, u32[]{:S(2)}) collective-permute-start(bf16[32,2048]{1,0:T(8,128)(2,1)S(1)} %pad_maximum_fusion), channel_id=1, source_target_pairs={{16,0},{17,1},{18,2},{19,3},{20,4},{21,5},{22,6},{23,7},{24,8},{25... | collective-permute-start | bytes 393224 | tf_op jit(solution)/shard_map/ppermute | solution.py:10
Sparse Core Ops, SparseCore 0:
  9.5 67.6 all-gather.5
  96.7 46.3 all-gather.3
